TPU v7x, 512 devices: a whole 4x4x16 slice. The times are simulated.
512 devices in a mesh: depth: 16 (over z), lat: 32 (over x, y, core).
Axes of the slice: x: 4, y: 4, z: 16, core: 2. Of those that a mesh axis runs over, the one named last changes fastest.
Arguments:
- volume: float32 [4, 64, 512, 512], P(None, 'depth', 'lat'), may hold values from 0 to 2
- offsets: int32 [8, 64], P(None, 'depth'), may hold values from -4 to 4, as said below
- view_ids: int32 [2], replicated, may hold values from 0 to 7
- weights: float32 [2, 4, 512, 512], P(None, None, 'lat'), may hold values from -6 to 6
Outputs:
- image_out: float32 [2, 4, 512, 512], P(None, None, 'lat')
- grad_out: float32 [4, 64, 512, 512], P(None, 'depth', 'lat')
Inputs may be any that keep to these rules, and one draw needn't show every extreme that they name: `offsets`: in every pose some slice has offset 4 and another has offset -4.
All inputs are finite; a program needn't handle non-finite values.
Results may differ from a plain program's by a relative error of at most 0.00017.
Values sent between devices are 32-bit elements; how exact they have to be, the bound alone decides.
No kernel may reach another device: no remote copies, remote signals or barrier semaphores. Data moves between devices by JAX's collectives and lax.ppermute only.
A program may use at most 64 MiB of HBM per device.

v0:
```python
import jax
import jax.numpy as jnp
from jax import lax
from jax.experimental import pallas as pl
from jax.experimental.pallas import tpu as pltpu
from jax.sharding import PartitionSpec as P


HALO = 4
LANES = 128
VMEM = pl.BlockSpec(memory_space=pltpu.VMEM)
SMEM = pl.BlockSpec(memory_space=pltpu.SMEM)
LIMIT = pltpu.CompilerParams(vmem_limit_bytes=16 * 1024 * 1024)


def fill_kernel(vol, ext):
    channels, slabs, rows, cols = vol.shape
    for c in range(channels):
        for k in range(slabs):
            for t in range(cols // LANES):
                ext[c, k, t, 8 : 8 + rows, :] = vol[c, k, :, pl.ds(t * LANES, LANES)]


def slab_kernel(
    depth_total, offs, vids, strip, place, inner, outer, own, w, agg, ext, absorb_part, emit_part
):
    del place, own
    channels, slabs, tiles, rows = ext.shape[:4]
    rows -= 16
    views = vids.shape[0]
    bands = rows // 8
    odd = lax.rem(strip[0], 2) == 1
    for c in range(channels):
        for k in range(slabs):
            for t in range(tiles):
                lanes = pl.ds(t * LANES, LANES)
                near, far = inner[c, k, :, lanes], outer[c, k, :, lanes]
                ext[c, k, t, 4:8, :] = jnp.where(odd, near, far)
                ext[c, k, t, 8 + rows : 12 + rows, :] = jnp.where(odd, far, near)
    for v in range(views):
        starts = [8 - offs[k, vids[v]] for k in range(slabs)]
        for t in range(tiles):
            lanes = pl.ds(t * LANES, LANES)
            weight = [w[v, c, :, lanes] for c in range(3)]
            transmit = jnp.ones((rows, LANES), jnp.float32)
            colour = [jnp.zeros((rows, LANES), jnp.float32) for _ in range(3)]
            alphas, keeps, glows, fronts = [], [], [], []
            for k in range(slabs):
                part = [ext[c, k, t, pl.ds(starts[k], rows), :] for c in range(channels)]
                keep = jnp.exp(part[3] * (-1.0 / depth_total))
                alpha = 1.0 - keep
                seen = transmit * alpha
                colour = [colour[c] + seen * part[c] for c in range(3)]
                emit_part[v, k, t] = seen * float(depth_total)
                glows.append(weight[0] * part[0] + weight[1] * part[1] + weight[2] * part[2])
                alphas.append(alpha)
                keeps.append(keep)
                transmit = transmit * keep
                fronts.append(transmit)
            behind = jnp.zeros((rows, LANES), jnp.float32)
            for k in range(slabs - 1, -1, -1):
                absorb_part[v, k, t] = fronts[k] * (glows[k] - behind)
                behind = alphas[k] * glows[k] + keeps[k] * behind
            for b in range(bands):
                owner = v * bands + b
                agg[owner, 0, t] = transmit[8 * b : 8 * b + 8]
                for c in range(3):
                    agg[owner, 1 + c, t] = colour[c][8 * b : 8 * b + 8]


def seat(place, members):
    mine, member = lax.div(place[0], members), lax.rem(place[0], members)
    turned = mine >= 2
    half = members // 2
    order = [jnp.where(turned, (j + half) % members, j) for j in range(members)]
    return mine, jnp.where(turned, lax.rem(member + half, members), member), order


def group_kernel(place, agg, out):
    members, _, tiles = agg.shape[:3]
    _, _, order = seat(place, members)
    for t in range(tiles):
        transmit = agg[order[0], 0, t]
        colour = [agg[order[0], 1 + c, t] for c in range(3)]
        for j in range(1, members):
            colour = [colour[c] + transmit * agg[order[j], 1 + c, t] for c in range(3)]
            transmit = transmit * agg[order[j], 0, t]
        out[0, t] = transmit
        for c in range(3):
            out[1 + c, t] = colour[c]


def scan_kernel(place, agg, *refs):
    parts, (w, out, shown) = refs[:-3], refs[-3:]
    members, _, tiles = agg.shape[:3]
    mine, owner, order = seat(place, members)
    bands = w.shape[2] // 8
    view, band = lax.div(owner, bands), lax.rem(owner, bands)
    rows = pl.ds(pl.multiple_of(8 * band, 8), 8)
    for t in range(tiles):
        lanes = pl.ds(t * LANES, LANES)
        weight = [w[view, c, rows, lanes] for c in range(4)]
        transmit = jnp.ones((8, LANES), jnp.float32)
        colour = [jnp.zeros((8, LANES), jnp.float32) for _ in range(3)]
        front = transmit
        count = len(parts)
        own = [[part[c, t] for c in range(4)] for part in parts]
        groups = []
        for g in range(count):
            found = own[g]
            for h in range(1, count):
                found = [jnp.where(mine == h, own[g ^ h][c], found[c]) for c in range(4)]
            groups.append(found)
        for g in range(count):
            front = jnp.where(mine == g, transmit, front)
            colour = [colour[c] + transmit * groups[g][1 + c] for c in range(3)]
            transmit = transmit * groups[g][0]
        picture = colour + [1.0 - transmit]
        behind = -weight[3]
        enter = behind
        for g in range(count - 1, 0, -1):
            glow = sum(weight[c] * groups[g][1 + c] for c in range(3))
            behind = glow + groups[g][0] * behind
            enter = jnp.where(mine == g - 1, behind, enter)
        fronts = []
        for j in range(members):
            fronts.append(front)
            front = front * agg[order[j], 0, t]
        for j in range(members - 1, -1, -1):
            passed = agg[order[j], 0, t] * enter
            out[order[j], 0, t] = fronts[j]
            out[order[j], 1, t] = fronts[j] * passed
            for c in range(4):
                shown[j, c, t] = picture[c]
            enter = passed + sum(weight[c] * agg[order[j], 1 + c, t] for c in range(3))


def pixel_grads(got, absorb_part, emit_part, w, v, t, bands, slabs):
    lanes = pl.ds(t * LANES, LANES)
    owners = [v * bands + b for b in range(bands)]
    front = jnp.concatenate([got[n, 0, t] for n in owners], axis=0)
    passed = jnp.concatenate([got[n, 1, t] for n in owners], axis=0)
    weight = [front * w[v, c, :, lanes] for c in range(3)]
    for k in range(slabs):
        emit = emit_part[v, k, t]
        parts = [emit * weight[c] for c in range(3)]
        parts.append(front * absorb_part[v, k, t] - passed)
        yield k, parts


def edge_kernel(offs, vids, strip, got, absorb_part, emit_part, w, inner, outer, shifted):
    views, channels, rows, cols = w.shape
    slabs = inner.shape[1]
    tiles = cols // LANES
    bands = rows // 8
    odd = lax.rem(strip[0], 2) == 1
    edge = jnp.zeros((8, LANES), jnp.float32)
    moves = [[offs[k, vids[v]] for k in range(slabs)] for v in range(views)]
    for t in range(tiles):
        lanes = pl.ds(t * LANES, LANES)
        for v in range(views):
            grads = pixel_grads(got, absorb_part, emit_part, w, v, t, bands, slabs)
            for k, parts in grads:
                for c in range(channels):
                    shifted[v, k, c, t, 0:8, :] = edge
                    shifted[v, k, c, t, 8 : 8 + rows, :] = parts[c]
                    shifted[v, k, c, t, 8 + rows : 16 + rows, :] = edge
        for k in range(slabs):
            for c in range(channels):

                def total(start):
                    return sum(
                        shifted[v, k, c, t, pl.ds(start + moves[v][k], 4), :]
                        for v in range(views)
                    )

                low, high = total(4), total(8 + rows)
                inner[c, k, :, lanes] = jnp.where(odd, low, high)
                outer[c, k, :, lanes] = jnp.where(odd, high, low)


def main_kernel(offs, vids, got, absorb_part, emit_part, w, main, shifted):
    views, channels, rows, cols = w.shape
    slabs = main.shape[1]
    tiles = cols // LANES
    bands = rows // 8
    edge = jnp.zeros((4, LANES), jnp.float32)
    moves = [[offs[k, vids[v]] for k in range(slabs)] for v in range(views)]
    for t in range(tiles):
        lanes = pl.ds(t * LANES, LANES)
        for v in range(views):
            grads = pixel_grads(got, absorb_part, emit_part, w, v, t, bands, slabs)
            for k, parts in grads:
                for c in range(channels):
                    shifted[v, k, c, t, 4:8, :] = edge
                    shifted[v, k, c, t, 8 : 8 + rows, :] = parts[c]
                    shifted[v, k, c, t, 8 + rows : 12 + rows, :] = edge
        for k in range(slabs):
            for c in range(channels):
                main[c, k, :, lanes] = sum(
                    shifted[v, k, c, t, pl.ds(8 + moves[v][k], rows), :] for v in range(views)
                )


def join_kernel(strip, main, inner, outer, shown, out, image):
    rows = main.shape[2]
    views, channels, _, cols = image.shape
    bands = rows // 8
    odd = lax.rem(strip[0], 2) == 1
    near, far = inner[...], outer[...]
    out[:, :, 0:4, :] = main[:, :, 0:4, :] + jnp.where(odd, near, far)
    out[:, :, 4 : rows - 4, :] = main[:, :, 4 : rows - 4, :]
    out[:, :, rows - 4 :, :] = main[:, :, rows - 4 :, :] + jnp.where(odd, far, near)
    for v in range(views):
        for b in range(bands):
            for t in range(cols // LANES):
                for c in range(channels):
                    image[v, c, 8 * b : 8 * b + 8, t * LANES : (t + 1) * LANES] = shown[
                        v * bands + b, c, t
                    ]


def off_chip(x):
    return pltpu.with_memory_space_constraint(x, pltpu.HBM)


def on_chip(x):
    return pltpu.with_memory_space_constraint(x, pltpu.VMEM)


def on_device(volume, offsets, view_ids, weights):
    channels, slabs, rows, cols = volume.shape
    views = weights.shape[0]
    count = lax.axis_size("depth")
    strips = lax.axis_size("lat")
    tiles, bands = cols // LANES, rows // 8
    depth_total = slabs * count
    size = views * bands
    near = [[size * g + i for i in range(size)] for g in range(count // size)]
    near = [row[size // 2 :] + row[: size // 2] if g >= 2 else row for g, row in enumerate(near)]
    pairs = [(i, i ^ 1) for i in range(strips)]
    links = [(i, ((i + 1) ^ 1) - 1) for i in range(1, strips - 1)]
    f32 = lambda *shape: jax.ShapeDtypeStruct(shape, jnp.float32)
    kept = lambda *shape: pltpu.VMEM(shape, jnp.float32)
    table, view_ids = off_chip(offsets.T), off_chip(view_ids)
    place = lax.axis_index("depth").reshape(1).astype(jnp.int32)
    w = on_chip(weights)

    def swap(x, groups):
        return lax.all_to_all(x, "depth", 0, 0, tiled=True, axis_index_groups=groups)

    strip = lax.axis_index("lat").reshape(1).astype(jnp.int32)
    odd = (strip & 1) == 1
    first, last = volume[:, :, :HALO], volume[:, :, rows - HALO :]
    outer = lax.ppermute(jnp.where(odd, last, first), "lat", links)
    inner = lax.ppermute(jnp.where(odd, first, last), "lat", pairs)
    own = pl.pallas_call(
        fill_kernel,
        out_shape=kept(channels, slabs, tiles, rows + 16, LANES),
        in_specs=[VMEM],
        out_specs=VMEM,
        compiler_params=LIMIT,
        name="fill",
    )(on_chip(volume))
    agg, _, absorb_part, emit_part = pl.pallas_call(
        lambda *refs: slab_kernel(depth_total, *refs),
        out_shape=(
            kept(size, 4, tiles, 8, LANES),
            kept(channels, slabs, tiles, rows + 16, LANES),
            kept(views, slabs, tiles, rows, LANES),
            kept(views, slabs, tiles, rows, LANES),
        ),
        in_specs=[SMEM, SMEM, SMEM, SMEM, VMEM, VMEM, VMEM, VMEM],
        out_specs=(VMEM, VMEM, VMEM, VMEM),
        input_output_aliases={6: 1},
        compiler_params=LIMIT,
        name="slab",
    )(table, view_ids, strip, place, on_chip(inner), on_chip(outer), on_chip(own), w)
    agg = on_chip(swap(agg, near))
    grouped = pl.pallas_call(
        group_kernel,
        out_shape=kept(4, tiles, 8, LANES),
        in_specs=[SMEM, VMEM],
        out_specs=VMEM,
        compiler_params=LIMIT,
        name="group",
    )(place, agg)
    parts = {0: grouped}
    for j in (2, 3, 1):
        hops = [(a, b) for g, row in enumerate(near) for a, b in zip(row, near[g ^ j])]
        parts[j] = lax.ppermute(grouped, "depth", hops)
    parts = [on_chip(parts[j]) for j in range(count // size)]
    sent, shown = pl.pallas_call(
        scan_kernel,
        out_shape=(kept(size, 2, tiles, 8, LANES), kept(size, 4, tiles, 8, LANES)),
        in_specs=[SMEM] + [VMEM] * (2 + count // size),
        out_specs=(VMEM, VMEM),
        compiler_params=LIMIT,
        name="scan",
    )(place, agg, *parts, w)
    got = on_chip(swap(sent, near))
    shown = swap(shown, near)

    to_inner, to_outer = pl.pallas_call(
        edge_kernel,
        out_shape=(
            kept(channels, slabs, HALO, cols),
            kept(channels, slabs, HALO, cols),
        ),
        in_specs=[SMEM, SMEM, SMEM, VMEM, VMEM, VMEM, VMEM],
        out_specs=(VMEM, VMEM),
        scratch_shapes=[
            pltpu.VMEM((views, slabs, channels, tiles, rows + 16, LANES), jnp.float32)
        ],
        compiler_params=LIMIT,
        name="edge",
    )(table, view_ids, strip, got, on_chip(absorb_part), on_chip(emit_part), w)
    from_outer = lax.ppermute(to_outer, "lat", links)
    from_inner = lax.ppermute(to_inner, "lat", pairs)
    main = pl.pallas_call(
        main_kernel,
        out_shape=kept(channels, slabs, rows, cols),
        in_specs=[SMEM, SMEM, VMEM, VMEM, VMEM, VMEM],
        out_specs=VMEM,
        scratch_shapes=[
            pltpu.VMEM((views, slabs, channels, tiles, rows + 16, LANES), jnp.float32)
        ],
        compiler_params=LIMIT,
        name="main",
    )(table, view_ids, got, on_chip(absorb_part), on_chip(emit_part), w)
    grad_out, image_out = pl.pallas_call(
        join_kernel,
        out_shape=(f32(channels, slabs, rows, cols), f32(views, channels, rows, cols)),
        in_specs=[SMEM, VMEM, VMEM, VMEM, VMEM],
        out_specs=(VMEM, VMEM),
        compiler_params=LIMIT,
        name="join",
    )(strip, on_chip(main), on_chip(from_inner), on_chip(from_outer), on_chip(shown))
    return (image_out, grad_out)


def solution(mesh):
    in_specs = (P(None, "depth", "lat", None), P(None, "depth"), P(), P(None, None, "lat", None))
    out_specs = (P(None, None, "lat", None), P(None, "depth", "lat", None))
    return jax.shard_map(
        on_device, mesh=mesh, in_specs=in_specs, out_specs=out_specs, check_vma=False
    )
```

profile of v0, /device:TPU:59, one launch (start us, length us, event | category | flops | bytes accessed | tf_op | source)
XLA Modules:
  0.0 80.2 jit_solution(12197385867873133938)
XLA Ops:
  0.6 0.0 copy-start.1
  0.6 1.1 %slice_select_fusion = (f32[4,4,4,512]{3,2,1,0:T(4,128)S(1)}, f32[4,4,4,512]{3,2,1,0:T(4,128)S(1)}) fusion(f32[4,4,16,512]{3,2,1,0:T(8,128)} %vol.1, pred[]{:T(512)} %bitcast.3), kind=kLoop, calls=%fused_computation | loop fusion | flops 65536 | bytes 524289 | tf_op jit(solution)/shard_map/jit(_where)/select_n | solution.py:255
  1.8 3.3 %collective-permute-start.1 = (f32[4,4,4,512]{3,2,1,0:T(4,128)S(1)}, f32[4,4,4,512]{3,2,1,0:T(4,128)S(1)}, u32[]{:S(2)}, u32[]{:S(2)}) collective-permute-start(f32[4,4,4,512]{3,2,1,0:T(4,128)S(1)} %get-tuple-element.20), channel_id=1, source_target_pairs={{1,2},{2,1},{3,4},{4,3},{5,6},{6,5},{7,8},{8,7},{9,10},{10,9},{11,... | collective-permute-start | bytes 393224 | tf_op jit(solution)/shard_map/ppermute | solution.py:255
  5.1 0.0 copy-start
  5.1 2.1 %collective-permute-start = (f32[4,4,4,512]{3,2,1,0:T(4,128)S(1)}, f32[4,4,4,512]{3,2,1,0:T(4,128)S(1)}, u32[]{:S(2)}, u32[]{:S(2)}) collective-permute-start(f32[4,4,4,512]{3,2,1,0:T(4,128)S(1)} %get-tuple-element.21), channel_id=1, source_target_pairs={{0,1},{1,0},{2,3},{3,2},{4,5},{5,4},{6,7},{7,6},{8,9},{9,8},{10,11... | collective-permute-start | bytes 393224 | tf_op jit(solution)/shard_map/ppermute | solution.py:256
  7.2 0.0 copy-done.1
  7.3 2.9 %collective-permute-done.1.refs_5_ = f32[4,4,4,512]{3,2,1,0:T(4,128)S(1)} collective-permute-done((f32[4,4,4,512]{3,2,1,0:T(4,128)S(1)}, f32[4,4,4,512]{3,2,1,0:T(4,128)S(1)}, u32[]{:S(2)}, u32[]{:S(2)}) %collective-permute-start.1) | collective-permute-done | bytes 131104 | tf_op jit(solution)/shard_map/ppermute | solution.py:255
  10.2 0.0 collective-permute-done.refs_4_
  10.2 0.0 copy-done
  10.2 1.0 %slab.1 = (f32[4,4,4,8,128]{4,3,2,1,0:T(8,128)S(1)}, f32[4,4,4,32,128]{4,3,2,1,0:T(8,128)S(1)}, f32[2,4,4,16,128]{4,3,2,1,0:T(8,128)S(1)}, f32[2,4,4,16,128]{4,3,2,1,0:T(8,128)S(1)}) custom-call(s32[4,8]{1,0:T(4,128)} %bitcast.4, s32[2]{0:T(128)} %vids.3, s32[1]{0:T(128)} %bitcast.refs_2_.strip, ...), custom_call_target="tpu_custom_call", output_to_operand_aliasing={{1}: (6, {})} | custom-call | tf_op jit(solution)/shard_map/slab/pallas_call | solution.py:265
  11.1 12.2 %all_to_all.15.agg = f32[4,4,4,8,128]{4,3,2,1,0:T(8,128)S(1)} all-to-all(f32[4,4,4,8,128]{4,3,2,1,0:T(8,128)S(1)} %get-tuple-element.11), channel_id=1, replica_groups={{0,32,64,96},{128,160,192,224},{320,352,256,288},{448,480,384,416},{1,3..., dimensions={0} | all-to-all | bytes 524288 | tf_op jit(solution)/shard_map/all_to_all | solution.py:250
  23.3 8.7 %collective-permute-start.4 = (f32[4,4,8,128]{3,2,1,0:T(8,128)S(1)}, f32[4,4,8,128]{3,2,1,0:T(8,128)S(1)}, u32[]{:S(2)}, u32[]{:S(2)}) collective-permute-start(f32[4,4,8,128]{3,2,1,0:T(8,128)S(1)} %group.1.refs_0_), channel_id=1, source_target_pairs={{0,448},{32,480},{64,384},{96,416},{128,320},{160,352},{192,256},{... | collective-permute-start | bytes 196616 | tf_op jit(solution)/shard_map/ppermute | solution.py:291
  32.1 7.1 %collective-permute-start.3 = (f32[4,4,8,128]{3,2,1,0:T(8,128)S(1)}, f32[4,4,8,128]{3,2,1,0:T(8,128)S(1)}, u32[]{:S(2)}, u32[]{:S(2)}) collective-permute-start(f32[4,4,8,128]{3,2,1,0:T(8,128)S(1)} %group.1.refs_0_), channel_id=1, source_target_pairs={{0,320},{32,352},{64,256},{96,288},{128,448},{160,480},{192,384},{... | collective-permute-start | bytes 196616 | tf_op jit(solution)/shard_map/ppermute | solution.py:291
  39.2 1.9 %collective-permute-start.2 = (f32[4,4,8,128]{3,2,1,0:T(8,128)S(1)}, f32[4,4,8,128]{3,2,1,0:T(8,128)S(1)}, u32[]{:S(2)}, u32[]{:S(2)}) collective-permute-start(f32[4,4,8,128]{3,2,1,0:T(8,128)S(1)} %group.1.refs_0_), channel_id=1, source_target_pairs={{0,128},{32,160},{64,192},{96,224},{128,0},{160,32},{192,64},{224,... | collective-permute-start | bytes 196616 | tf_op jit(solution)/shard_map/ppermute | solution.py:291
  41.1 0.0 collective-permute-done.4.refs_3_
  41.1 6.7 %collective-permute-done.3.refs_2_ = f32[4,4,8,128]{3,2,1,0:T(8,128)S(1)} collective-permute-done((f32[4,4,8,128]{3,2,1,0:T(8,128)S(1)}, f32[4,4,8,128]{3,2,1,0:T(8,128)S(1)}, u32[]{:S(2)}, u32[]{:S(2)}) %collective-permute-start.3) | collective-permute-done | bytes 65568 | tf_op jit(solution)/shard_map/ppermute | solution.py:291
  47.8 3.8 %collective-permute-done.2.refs_1_ = f32[4,4,8,128]{3,2,1,0:T(8,128)S(1)} collective-permute-done((f32[4,4,8,128]{3,2,1,0:T(8,128)S(1)}, f32[4,4,8,128]{3,2,1,0:T(8,128)S(1)}, u32[]{:S(2)}, u32[]{:S(2)}) %collective-permute-start.2) | collective-permute-done | bytes 65568 | tf_op jit(solution)/shard_map/ppermute | solution.py:291
  51.6 0.8 scan.1
  52.4 9.4 %all_to_all.16.got = f32[4,2,4,8,128]{4,3,2,1,0:T(8,128)S(1)} all-to-all(f32[4,2,4,8,128]{4,3,2,1,0:T(8,128)S(1)} %get-tuple-element.12), channel_id=1, replica_groups={{0,32,64,96},{128,160,192,224},{320,352,256,288},{448,480,384,416},{1,3..., dimensions={0} | all-to-all | bytes 262144 | tf_op jit(solution)/shard_map/all_to_all | solution.py:250
  61.8 4.0 %all-to-all-start.2 = ((f32[4,4,4,8,128]{4,3,2,1,0:T(8,128)}), f32[4,4,4,8,128]{4,3,2,1,0:T(8,128)S(1)}, u32[]{:S(2)}, u32[]{:S(2)}) async-start(f32[4,4,4,8,128]{4,3,2,1,0:T(8,128)} %get-tuple-element.17), calls=%async_computation.2 | async-start | bytes 524288 | tf_op jit(solution)/shard_map/all_to_all | solution.py:250
  65.8 0.9 %edge.1 = (f32[4,4,4,512]{3,2,1,0:T(4,128)S(1)}, f32[4,4,4,512]{3,2,1,0:T(4,128)S(1)}) custom-call(s32[4,8]{1,0:T(4,128)} %bitcast.5, s32[2]{0:T(128)} %vids.3, s32[1]{0:T(128)} %bitcast.refs_2_.strip, f32[4,2,4,8,128]{4,3,2,1,0:T(8,128)S(1)} %all_to_all.16.got, f32[2,4,4,16,128]{4,3,2,1,0:T(8,128)S(1)} %get-tuple-element.13.absorb_part, ...), custom_call_target="tpu_custom_call" | custom-call | tf_op jit(solution)/shard_map/edge/pallas_call | solution.py:304
  66.7 4.0 %collective-permute-start.5 = (f32[4,4,4,512]{3,2,1,0:T(4,128)S(1)}, f32[4,4,4,512]{3,2,1,0:T(4,128)S(1)}, u32[]{:S(2)}, u32[]{:S(2)}) collective-permute-start(f32[4,4,4,512]{3,2,1,0:T(4,128)S(1)} %get-tuple-element.15), channel_id=1, source_target_pairs={{0,1},{1,0},{2,3},{3,2},{4,5},{5,4},{6,7},{7,6},{8,9},{9,8},{10,11... | collective-permute-start | bytes 393224 | tf_op jit(solution)/shard_map/ppermute | solution.py:319
  70.8 2.1 %collective-permute-start.6 = (f32[4,4,4,512]{3,2,1,0:T(4,128)S(1)}, f32[4,4,4,512]{3,2,1,0:T(4,128)S(1)}, u32[]{:S(2)}, u32[]{:S(2)}) collective-permute-start(f32[4,4,4,512]{3,2,1,0:T(4,128)S(1)} %get-tuple-element.16), channel_id=1, source_target_pairs={{1,2},{2,1},{3,4},{4,3},{5,6},{6,5},{7,8},{8,7},{9,10},{10,9},{11,... | collective-permute-start | bytes 393224 | tf_op jit(solution)/shard_map/ppermute | solution.py:318
  72.9 0.9 %main.1 = f32[4,4,16,512]{3,2,1,0:T(8,128)S(1)} custom-call(s32[4,8]{1,0:T(4,128)} %bitcast.6, s32[2]{0:T(128)} %vids.3, f32[4,2,4,8,128]{4,3,2,1,0:T(8,128)S(1)} %all_to_all.16.got, f32[2,4,4,16,128]{4,3,2,1,0:T(8,128)S(1)} %get-tuple-element.13.absorb_part, f32[2,4,4,16,128]{4,3,2,1,0:T(8,128)S(1)} %get-tuple-element.14.emit_part, ...), custom_call_target="tpu_custom_call" | custom-call | tf_op jit(solution)/shard_map/main/pallas_call | solution.py:320
  73.9 0.0 collective-permute-done.5.inner
  73.9 5.3 %collective-permute-done.6.outer = f32[4,4,4,512]{3,2,1,0:T(4,128)S(1)} collective-permute-done((f32[4,4,4,512]{3,2,1,0:T(4,128)S(1)}, f32[4,4,4,512]{3,2,1,0:T(4,128)S(1)}, u32[]{:S(2)}, u32[]{:S(2)}) %collective-permute-start.6) | collective-permute-done | bytes 131104 | tf_op jit(solution)/shard_map/ppermute | solution.py:318
  79.2 0.0 all-to-all-done.2.shown
  79.2 1.0 %join.1 = (f32[4,4,16,512]{3,2,1,0:T(8,128)}, f32[2,4,16,512]{3,2,1,0:T(8,128)}) custom-call(s32[1]{0:T(128)} %bitcast.refs_2_.strip, f32[4,4,16,512]{3,2,1,0:T(8,128)S(1)} %main.1, f32[4,4,4,512]{3,2,1,0:T(4,128)S(1)} %collective-permute-done.5.inner, f32[4,4,4,512]{3,2,1,0:T(4,128)S(1)} %collective-permute-done.6.outer, ...), custom_call_target="tpu_custom_call" | custom-call | tf_op jit(solution)/shard_map/join/pallas_call | solution.py:331
  (2 shorter events, 0.1 us)
Async XLA Ops:
  0.6 6.6 %copy-start.1 = (f32[4,4,16,512]{3,2,1,0:T(8,128)S(1)}, f32[4,4,16,512]{3,2,1,0:T(8,128)}, u32[]{:S(2)}) copy-start(f32[4,4,16,512]{3,2,1,0:T(8,128)} %vol.1) | copy-start | bytes 1572868
  1.8 8.4 %collective-permute-start.1 = (f32[4,4,4,512]{3,2,1,0:T(4,128)S(1)}, f32[4,4,4,512]{3,2,1,0:T(4,128)S(1)}, u32[]{:S(2)}, u32[]{:S(2)}) collective-permute-start(f32[4,4,4,512]{3,2,1,0:T(4,128)S(1)} %get-tuple-element.20), channel_id=1, source_target_pairs={{1,2},{2,1},{3,4},{4,3},{5,6},{6,5},{7,8},{8,7},{9,10},{10,9},{11,... | collective-permute-start | bytes 393224 | tf_op jit(solution)/shard_map/ppermute | solution.py:255
  5.1 5.1 %copy-start = (f32[2,4,16,512]{3,2,1,0:T(8,128)S(1)}, f32[2,4,16,512]{3,2,1,0:T(8,128)}, u32[]{:S(2)}) copy-start(f32[2,4,16,512]{3,2,1,0:T(8,128)} %w.3) | copy-start | bytes 786436
  5.1 5.0 %collective-permute-start = (f32[4,4,4,512]{3,2,1,0:T(4,128)S(1)}, f32[4,4,4,512]{3,2,1,0:T(4,128)S(1)}, u32[]{:S(2)}, u32[]{:S(2)}) collective-permute-start(f32[4,4,4,512]{3,2,1,0:T(4,128)S(1)} %get-tuple-element.21), channel_id=1, source_target_pairs={{0,1},{1,0},{2,3},{3,2},{4,5},{5,4},{6,7},{7,6},{8,9},{9,8},{10,11... | collective-permute-start | bytes 393224 | tf_op jit(solution)/shard_map/ppermute | solution.py:256
  23.3 17.8 %collective-permute-start.4 = (f32[4,4,8,128]{3,2,1,0:T(8,128)S(1)}, f32[4,4,8,128]{3,2,1,0:T(8,128)S(1)}, u32[]{:S(2)}, u32[]{:S(2)}) collective-permute-start(f32[4,4,8,128]{3,2,1,0:T(8,128)S(1)} %group.1.refs_0_), channel_id=1, source_target_pairs={{0,448},{32,480},{64,384},{96,416},{128,320},{160,352},{192,256},{... | collective-permute-start | bytes 196616 | tf_op jit(solution)/shard_map/ppermute | solution.py:291
  32.1 15.8 %collective-permute-start.3 = (f32[4,4,8,128]{3,2,1,0:T(8,128)S(1)}, f32[4,4,8,128]{3,2,1,0:T(8,128)S(1)}, u32[]{:S(2)}, u32[]{:S(2)}) collective-permute-start(f32[4,4,8,128]{3,2,1,0:T(8,128)S(1)} %group.1.refs_0_), channel_id=1, source_target_pairs={{0,320},{32,352},{64,256},{96,288},{128,448},{160,480},{192,384},{... | collective-permute-start | bytes 196616 | tf_op jit(solution)/shard_map/ppermute | solution.py:291
  39.2 12.5 %collective-permute-start.2 = (f32[4,4,8,128]{3,2,1,0:T(8,128)S(1)}, f32[4,4,8,128]{3,2,1,0:T(8,128)S(1)}, u32[]{:S(2)}, u32[]{:S(2)}) collective-permute-start(f32[4,4,8,128]{3,2,1,0:T(8,128)S(1)} %group.1.refs_0_), channel_id=1, source_target_pairs={{0,128},{32,160},{64,192},{96,224},{128,0},{160,32},{192,64},{224,... | collective-permute-start | bytes 196616 | tf_op jit(solution)/shard_map/ppermute | solution.py:291
  61.8 17.3 %all-to-all-start.2 = ((f32[4,4,4,8,128]{4,3,2,1,0:T(8,128)}), f32[4,4,4,8,128]{4,3,2,1,0:T(8,128)S(1)}, u32[]{:S(2)}, u32[]{:S(2)}) async-start(f32[4,4,4,8,128]{4,3,2,1,0:T(8,128)} %get-tuple-element.17), calls=%async_computation.2 | async-start | bytes 524288 | tf_op jit(solution)/shard_map/all_to_all | solution.py:250
  66.7 7.1 %collective-permute-start.5 = (f32[4,4,4,512]{3,2,1,0:T(4,128)S(1)}, f32[4,4,4,512]{3,2,1,0:T(4,128)S(1)}, u32[]{:S(2)}, u32[]{:S(2)}) collective-permute-start(f32[4,4,4,512]{3,2,1,0:T(4,128)S(1)} %get-tuple-element.15), channel_id=1, source_target_pairs={{0,1},{1,0},{2,3},{3,2},{4,5},{5,4},{6,7},{7,6},{8,9},{9,8},{10,11... | collective-permute-start | bytes 393224 | tf_op jit(solution)/shard_map/ppermute | solution.py:319
  70.8 8.4 %collective-permute-start.6 = (f32[4,4,4,512]{3,2,1,0:T(4,128)S(1)}, f32[4,4,4,512]{3,2,1,0:T(4,128)S(1)}, u32[]{:S(2)}, u32[]{:S(2)}) collective-permute-start(f32[4,4,4,512]{3,2,1,0:T(4,128)S(1)} %get-tuple-element.16), channel_id=1, source_target_pairs={{1,2},{2,1},{3,4},{4,3},{5,6},{6,5},{7,8},{8,7},{9,10},{10,9},{11,... | collective-permute-start | bytes 393224 | tf_op jit(solution)/shard_map/ppermute | solution.py:318
where the time goes:
time: 80.7 us; the launch traced here: 80.2 us
  starting transfers between devices  33.3 us (41%)
  blocking collectives  21.5 us (27%)
  waiting for transfers between devices  18.8 us (23%)
  Pallas kernels  4.66 us (6%)
  other arithmetic  1.14 us (1%)
    all_to_all x2, blocking collectives, swap(): lax.all_to_all(x, 'depth', 0, 0, tiled=True, axis_index_groups=groups)  21.5 us
    ppermute x3, starting transfers between devices, on_device(): parts[j] = lax.ppermute(grouped, 'depth', hops)  17.7 us
    ppermute x3, waiting for transfers between devices, on_device(): parts[j] = lax.ppermute(grouped, 'depth', hops)  10.6 us
    ppermute x1, waiting for transfers between devices, on_device(): from_outer = lax.ppermute(to_outer, 'lat', links)  5.28 us
    ppermute x1, starting transfers between devices, on_device(): from_inner = lax.ppermute(to_inner, 'lat', pairs)  4.02 us
    all_to_all x1, starting transfers between devices, swap(): lax.all_to_all(x, 'depth', 0, 0, tiled=True, axis_index_groups=groups)  3.99 us
    ppermute x1, starting transfers between devices, on_device(): outer = lax.ppermute(jnp.where(odd, last, first), 'lat', links)  3.34 us
    ppermute x1, waiting for transfers between devices, on_device(): outer = lax.ppermute(jnp.where(odd, last, first), 'lat', links)  2.92 us
  transfers between devices with their start and end apart: 8, of which 4 were waited for; matrix products, arithmetic and copies ran while one was open for 0% of the time, Pallas kernels for 2%

commit v1 on v0

--- a/solution.py
+++ b/solution.py
@@ -91,7 +91,7 @@
 
 
 def scan_kernel(place, agg, *refs):
-    parts, (w, out, shown) = refs[:-3], refs[-3:]
+    parts, (w, out) = refs[:-2], refs[-2:]
     members, _, tiles = agg.shape[:3]
     mine, owner, order = seat(place, members)
     bands = w.shape[2] // 8
@@ -131,7 +131,7 @@
             out[order[j], 0, t] = fronts[j]
             out[order[j], 1, t] = fronts[j] * passed
             for c in range(4):
-                shown[j, c, t] = picture[c]
+                out[order[j], 2 + c, t] = picture[c]
             enter = passed + sum(weight[c] * agg[order[j], 1 + c, t] for c in range(3))
 
 
@@ -216,7 +216,7 @@
             for t in range(cols // LANES):
                 for c in range(channels):
                     image[v, c, 8 * b : 8 * b + 8, t * LANES : (t + 1) * LANES] = shown[
-                        v * bands + b, c, t
+                        v * bands + b, 2 + c, t
                     ]
 
 
@@ -290,16 +290,16 @@
         hops = [(a, b) for g, row in enumerate(near) for a, b in zip(row, near[g ^ j])]
         parts[j] = lax.ppermute(grouped, "depth", hops)
     parts = [on_chip(parts[j]) for j in range(count // size)]
-    sent, shown = pl.pallas_call(
+    sent = pl.pallas_call(
         scan_kernel,
-        out_shape=(kept(size, 2, tiles, 8, LANES), kept(size, 4, tiles, 8, LANES)),
+        out_shape=kept(size, 6, tiles, 8, LANES),
         in_specs=[SMEM] + [VMEM] * (2 + count // size),
-        out_specs=(VMEM, VMEM),
+        out_specs=VMEM,
         compiler_params=LIMIT,
         name="scan",
     )(place, agg, *parts, w)
     got = on_chip(swap(sent, near))
-    shown = swap(shown, near)
+    shown = got
 
     to_inner, to_outer = pl.pallas_call(
         edge_kernel,

time: 80.7 us -> 82.2 us (1.019)
  the two profiles are of different devices: /device:TPU:59 before, /device:TPU:25 now
where the time goes in v1:
time: 82.2 us; the launch traced here: 81.8 us
  starting transfers between devices  28.5 us (35%)
  blocking collectives  27.6 us (34%)
  waiting for transfers between devices  19.8 us (24%)
  Pallas kernels  3.99 us (5%)
  other arithmetic  1.14 us (1%)
    all_to_all x2, blocking collectives, swap(): lax.all_to_all(x, 'depth', 0, 0, tiled=True, axis_index_groups=groups)  27.6 us
    ppermute x3, starting transfers between devices, on_device(): parts[j] = lax.ppermute(grouped, 'depth', hops)  17.7 us
    ppermute x3, waiting for transfers between devices, on_device(): parts[j] = lax.ppermute(grouped, 'depth', hops)  11.6 us
    ppermute x1, waiting for transfers between devices, on_device(): from_outer = lax.ppermute(to_outer, 'lat', links)  5.29 us
    ppermute x1, starting transfers between devices, on_device(): outer = lax.ppermute(jnp.where(odd, last, first), 'lat', links)  3.34 us
    ppermute x1, starting transfers between devices, on_device(): from_inner = lax.ppermute(to_inner, 'lat', pairs)  3.21 us
    ppermute x1, waiting for transfers between devices, on_device(): outer = lax.ppermute(jnp.where(odd, last, first), 'lat', links)  2.92 us
    ppermute x1, starting transfers between devices, on_device(): from_outer = lax.ppermute(to_outer, 'lat', links)  2.13 us
  transfers between devices with their start and end apart: 7, of which 4 were waited for; matrix products, arithmetic and copies ran while one was open for 0% of the time, Pallas kernels for 1%

profile of v1, /device:TPU:25, one launch (start us, length us, event | category | flops | bytes accessed | tf_op | source)
XLA Modules:
  0.0 81.8 jit_solution(1060932966071724194)
XLA Ops:
  0.6 0.0 copy-start.1
  0.6 1.1 %slice_select_fusion = (f32[4,4,4,512]{3,2,1,0:T(4,128)S(1)}, f32[4,4,4,512]{3,2,1,0:T(4,128)S(1)}) fusion(f32[4,4,16,512]{3,2,1,0:T(8,128)} %vol.1, pred[]{:T(512)} %bitcast.3), kind=kLoop, calls=%fused_computation | loop fusion | flops 65536 | bytes 524289 | tf_op jit(solution)/shard_map/jit(_where)/select_n | solution.py:255
  1.8 3.3 %collective-permute-start.1 = (f32[4,4,4,512]{3,2,1,0:T(4,128)S(1)}, f32[4,4,4,512]{3,2,1,0:T(4,128)S(1)}, u32[]{:S(2)}, u32[]{:S(2)}) collective-permute-start(f32[4,4,4,512]{3,2,1,0:T(4,128)S(1)} %get-tuple-element.16), channel_id=1, source_target_pairs={{1,2},{2,1},{3,4},{4,3},{5,6},{6,5},{7,8},{8,7},{9,10},{10,9},{11,... | collective-permute-start | bytes 393224 | tf_op jit(solution)/shard_map/ppermute | solution.py:255
  5.1 0.0 copy-start
  5.1 2.1 %collective-permute-start = (f32[4,4,4,512]{3,2,1,0:T(4,128)S(1)}, f32[4,4,4,512]{3,2,1,0:T(4,128)S(1)}, u32[]{:S(2)}, u32[]{:S(2)}) collective-permute-start(f32[4,4,4,512]{3,2,1,0:T(4,128)S(1)} %get-tuple-element.17), channel_id=1, source_target_pairs={{0,1},{1,0},{2,3},{3,2},{4,5},{5,4},{6,7},{7,6},{8,9},{9,8},{10,11... | collective-permute-start | bytes 393224 | tf_op jit(solution)/shard_map/ppermute | solution.py:256
  7.2 0.0 copy-done.1
  7.3 2.9 %collective-permute-done.1.refs_5_ = f32[4,4,4,512]{3,2,1,0:T(4,128)S(1)} collective-permute-done((f32[4,4,4,512]{3,2,1,0:T(4,128)S(1)}, f32[4,4,4,512]{3,2,1,0:T(4,128)S(1)}, u32[]{:S(2)}, u32[]{:S(2)}) %collective-permute-start.1) | collective-permute-done | bytes 131104 | tf_op jit(solution)/shard_map/ppermute | solution.py:255
  10.2 0.0 collective-permute-done.refs_4_
  10.2 0.0 copy-done
  10.2 1.0 %slab.1 = (f32[4,4,4,8,128]{4,3,2,1,0:T(8,128)S(1)}, f32[4,4,4,32,128]{4,3,2,1,0:T(8,128)S(1)}, f32[2,4,4,16,128]{4,3,2,1,0:T(8,128)S(1)}, f32[2,4,4,16,128]{4,3,2,1,0:T(8,128)S(1)}) custom-call(s32[4,8]{1,0:T(4,128)} %bitcast.4, s32[2]{0:T(128)} %vids.3, s32[1]{0:T(128)} %bitcast.refs_2_.strip, ...), custom_call_target="tpu_custom_call", output_to_operand_aliasing={{1}: (6, {})} | custom-call | tf_op jit(solution)/shard_map/slab/pallas_call | solution.py:265
  11.2 13.9 %all_to_all.10.agg = f32[4,4,4,8,128]{4,3,2,1,0:T(8,128)S(1)} all-to-all(f32[4,4,4,8,128]{4,3,2,1,0:T(8,128)S(1)} %get-tuple-element.9), channel_id=1, replica_groups={{0,32,64,96},{128,160,192,224},{320,352,256,288},{448,480,384,416},{1,3..., dimensions={0} | all-to-all | bytes 524288 | tf_op jit(solution)/shard_map/all_to_all | solution.py:250
  25.0 7.1 %collective-permute-start.4 = (f32[4,4,8,128]{3,2,1,0:T(8,128)S(1)}, f32[4,4,8,128]{3,2,1,0:T(8,128)S(1)}, u32[]{:S(2)}, u32[]{:S(2)}) collective-permute-start(f32[4,4,8,128]{3,2,1,0:T(8,128)S(1)} %group.1.refs_0_), channel_id=1, source_target_pairs={{0,448},{32,480},{64,384},{96,416},{128,320},{160,352},{192,256},{... | collective-permute-start | bytes 196616 | tf_op jit(solution)/shard_map/ppermute | solution.py:291
  32.2 8.7 %collective-permute-start.3 = (f32[4,4,8,128]{3,2,1,0:T(8,128)S(1)}, f32[4,4,8,128]{3,2,1,0:T(8,128)S(1)}, u32[]{:S(2)}, u32[]{:S(2)}) collective-permute-start(f32[4,4,8,128]{3,2,1,0:T(8,128)S(1)} %group.1.refs_0_), channel_id=1, source_target_pairs={{0,320},{32,352},{64,256},{96,288},{128,448},{160,480},{192,384},{... | collective-permute-start | bytes 196616 | tf_op jit(solution)/shard_map/ppermute | solution.py:291
  40.9 1.9 %collective-permute-start.2 = (f32[4,4,8,128]{3,2,1,0:T(8,128)S(1)}, f32[4,4,8,128]{3,2,1,0:T(8,128)S(1)}, u32[]{:S(2)}, u32[]{:S(2)}) collective-permute-start(f32[4,4,8,128]{3,2,1,0:T(8,128)S(1)} %group.1.refs_0_), channel_id=1, source_target_pairs={{0,128},{32,160},{64,192},{96,224},{128,0},{160,32},{192,64},{224,... | collective-permute-start | bytes 196616 | tf_op jit(solution)/shard_map/ppermute | solution.py:291
  42.8 0.0 collective-permute-done.4.refs_3_
  42.8 2.1 %collective-permute-done.3.refs_2_ = f32[4,4,8,128]{3,2,1,0:T(8,128)S(1)} collective-permute-done((f32[4,4,8,128]{3,2,1,0:T(8,128)S(1)}, f32[4,4,8,128]{3,2,1,0:T(8,128)S(1)}, u32[]{:S(2)}, u32[]{:S(2)}) %collective-permute-start.3) | collective-permute-done | bytes 65568 | tf_op jit(solution)/shard_map/ppermute | solution.py:291
  44.9 9.5 %collective-permute-done.2.refs_1_ = f32[4,4,8,128]{3,2,1,0:T(8,128)S(1)} collective-permute-done((f32[4,4,8,128]{3,2,1,0:T(8,128)S(1)}, f32[4,4,8,128]{3,2,1,0:T(8,128)S(1)}, u32[]{:S(2)}, u32[]{:S(2)}) %collective-permute-start.2) | collective-permute-done | bytes 65568 | tf_op jit(solution)/shard_map/ppermute | solution.py:291
  54.4 0.1 scan.1
  54.5 13.7 %all_to_all.11.got.shown = f32[4,6,4,8,128]{4,3,2,1,0:T(8,128)S(1)} all-to-all(f32[4,6,4,8,128]{4,3,2,1,0:T(8,128)S(1)} %scan.1), channel_id=1, replica_groups={{0,32,64,96},{128,160,192,224},{320,352,256,288},{448,480,384,416},{1,3..., dimensions={0} | all-to-all | bytes 786432 | tf_op jit(solution)/shard_map/all_to_all | solution.py:250
  68.2 0.9 %edge.1 = (f32[4,4,4,512]{3,2,1,0:T(4,128)S(1)}, f32[4,4,4,512]{3,2,1,0:T(4,128)S(1)}) custom-call(s32[4,8]{1,0:T(4,128)} %bitcast.5, s32[2]{0:T(128)} %vids.3, s32[1]{0:T(128)} %bitcast.refs_2_.strip, f32[4,6,4,8,128]{4,3,2,1,0:T(8,128)S(1)} %all_to_all.11.got.shown, f32[2,4,4,16,128]{4,3,2,1,0:T(8,128)S(1)} %get-tuple-element.10.absorb_part, ...), custom_call_target="tpu_custom_call" | custom-call | tf_op jit(solution)/shard_map/edge/pallas_call | solution.py:304
  69.2 3.2 %collective-permute-start.5 = (f32[4,4,4,512]{3,2,1,0:T(4,128)S(1)}, f32[4,4,4,512]{3,2,1,0:T(4,128)S(1)}, u32[]{:S(2)}, u32[]{:S(2)}) collective-permute-start(f32[4,4,4,512]{3,2,1,0:T(4,128)S(1)} %get-tuple-element.12), channel_id=1, source_target_pairs={{0,1},{1,0},{2,3},{3,2},{4,5},{5,4},{6,7},{7,6},{8,9},{9,8},{10,11... | collective-permute-start | bytes 393224 | tf_op jit(solution)/shard_map/ppermute | solution.py:319
  72.4 2.1 %collective-permute-start.6 = (f32[4,4,4,512]{3,2,1,0:T(4,128)S(1)}, f32[4,4,4,512]{3,2,1,0:T(4,128)S(1)}, u32[]{:S(2)}, u32[]{:S(2)}) collective-permute-start(f32[4,4,4,512]{3,2,1,0:T(4,128)S(1)} %get-tuple-element.13), channel_id=1, source_target_pairs={{1,2},{2,1},{3,4},{4,3},{5,6},{6,5},{7,8},{8,7},{9,10},{10,9},{11,... | collective-permute-start | bytes 393224 | tf_op jit(solution)/shard_map/ppermute | solution.py:318
  74.5 1.0 %main.1 = f32[4,4,16,512]{3,2,1,0:T(8,128)S(1)} custom-call(s32[4,8]{1,0:T(4,128)} %bitcast.6, s32[2]{0:T(128)} %vids.3, f32[4,6,4,8,128]{4,3,2,1,0:T(8,128)S(1)} %all_to_all.11.got.shown, f32[2,4,4,16,128]{4,3,2,1,0:T(8,128)S(1)} %get-tuple-element.10.absorb_part, f32[2,4,4,16,128]{4,3,2,1,0:T(8,128)S(1)} %get-tuple-element.11.emit_part, ...), custom_call_target="tpu_custom_call" | custom-call | tf_op jit(solution)/shard_map/main/pallas_call | solution.py:320
  75.5 0.0 collective-permute-done.5.inner
  75.5 5.3 %collective-permute-done.6.outer = f32[4,4,4,512]{3,2,1,0:T(4,128)S(1)} collective-permute-done((f32[4,4,4,512]{3,2,1,0:T(4,128)S(1)}, f32[4,4,4,512]{3,2,1,0:T(4,128)S(1)}, u32[]{:S(2)}, u32[]{:S(2)}) %collective-permute-start.6) | collective-permute-done | bytes 131104 | tf_op jit(solution)/shard_map/ppermute | solution.py:318
  80.8 1.0 %join.1 = (f32[4,4,16,512]{3,2,1,0:T(8,128)}, f32[2,4,16,512]{3,2,1,0:T(8,128)}) custom-call(s32[1]{0:T(128)} %bitcast.refs_2_.strip, f32[4,4,16,512]{3,2,1,0:T(8,128)S(1)} %main.1, f32[4,4,4,512]{3,2,1,0:T(4,128)S(1)} %collective-permute-done.5.inner, f32[4,4,4,512]{3,2,1,0:T(4,128)S(1)} %collective-permute-done.6.outer, ...), custom_call_target="tpu_custom_call" | custom-call | tf_op jit(solution)/shard_map/join/pallas_call | solution.py:331
  (2 shorter events, 0.1 us)
Async XLA Ops:
  0.6 6.6 %copy-start.1 = (f32[4,4,16,512]{3,2,1,0:T(8,128)S(1)}, f32[4,4,16,512]{3,2,1,0:T(8,128)}, u32[]{:S(2)}) copy-start(f32[4,4,16,512]{3,2,1,0:T(8,128)} %vol.1) | copy-start | bytes 1572868
  1.8 8.4 %collective-permute-start.1 = (f32[4,4,4,512]{3,2,1,0:T(4,128)S(1)}, f32[4,4,4,512]{3,2,1,0:T(4,128)S(1)}, u32[]{:S(2)}, u32[]{:S(2)}) collective-permute-start(f32[4,4,4,512]{3,2,1,0:T(4,128)S(1)} %get-tuple-element.16), channel_id=1, source_target_pairs={{1,2},{2,1},{3,4},{4,3},{5,6},{6,5},{7,8},{8,7},{9,10},{10,9},{11,... | collective-permute-start | bytes 393224 | tf_op jit(solution)/shard_map/ppermute | solution.py:255
  5.1 5.1 %copy-start = (f32[2,4,16,512]{3,2,1,0:T(8,128)S(1)}, f32[2,4,16,512]{3,2,1,0:T(8,128)}, u32[]{:S(2)}) copy-start(f32[2,4,16,512]{3,2,1,0:T(8,128)} %w.3) | copy-start | bytes 786436
  5.1 5.0 %collective-permute-start = (f32[4,4,4,512]{3,2,1,0:T(4,128)S(1)}, f32[4,4,4,512]{3,2,1,0:T(4,128)S(1)}, u32[]{:S(2)}, u32[]{:S(2)}) collective-permute-start(f32[4,4,4,512]{3,2,1,0:T(4,128)S(1)} %get-tuple-element.17), channel_id=1, source_target_pairs={{0,1},{1,0},{2,3},{3,2},{4,5},{5,4},{6,7},{7,6},{8,9},{9,8},{10,11... | collective-permute-start | bytes 393224 | tf_op jit(solution)/shard_map/ppermute | solution.py:256
  25.0 17.8 %collective-permute-start.4 = (f32[4,4,8,128]{3,2,1,0:T(8,128)S(1)}, f32[4,4,8,128]{3,2,1,0:T(8,128)S(1)}, u32[]{:S(2)}, u32[]{:S(2)}) collective-permute-start(f32[4,4,8,128]{3,2,1,0:T(8,128)S(1)} %group.1.refs_0_), channel_id=1, source_target_pairs={{0,448},{32,480},{64,384},{96,416},{128,320},{160,352},{192,256},{... | collective-permute-start | bytes 196616 | tf_op jit(solution)/shard_map/ppermute | solution.py:291
  32.2 12.7 %collective-permute-start.3 = (f32[4,4,8,128]{3,2,1,0:T(8,128)S(1)}, f32[4,4,8,128]{3,2,1,0:T(8,128)S(1)}, u32[]{:S(2)}, u32[]{:S(2)}) collective-permute-start(f32[4,4,8,128]{3,2,1,0:T(8,128)S(1)} %group.1.refs_0_), channel_id=1, source_target_pairs={{0,320},{32,352},{64,256},{96,288},{128,448},{160,480},{192,384},{... | collective-permute-start | bytes 196616 | tf_op jit(solution)/shard_map/ppermute | solution.py:291
  40.9 13.5 %collective-permute-start.2 = (f32[4,4,8,128]{3,2,1,0:T(8,128)S(1)}, f32[4,4,8,128]{3,2,1,0:T(8,128)S(1)}, u32[]{:S(2)}, u32[]{:S(2)}) collective-permute-start(f32[4,4,8,128]{3,2,1,0:T(8,128)S(1)} %group.1.refs_0_), channel_id=1, source_target_pairs={{0,128},{32,160},{64,192},{96,224},{128,0},{160,32},{192,64},{224,... | collective-permute-start | bytes 196616 | tf_op jit(solution)/shard_map/ppermute | solution.py:291
  69.2 6.3 %collective-permute-start.5 = (f32[4,4,4,512]{3,2,1,0:T(4,128)S(1)}, f32[4,4,4,512]{3,2,1,0:T(4,128)S(1)}, u32[]{:S(2)}, u32[]{:S(2)}) collective-permute-start(f32[4,4,4,512]{3,2,1,0:T(4,128)S(1)} %get-tuple-element.12), channel_id=1, source_target_pairs={{0,1},{1,0},{2,3},{3,2},{4,5},{5,4},{6,7},{7,6},{8,9},{9,8},{10,11... | collective-permute-start | bytes 393224 | tf_op jit(solution)/shard_map/ppermute | solution.py:319
  72.4 8.4 %collective-permute-start.6 = (f32[4,4,4,512]{3,2,1,0:T(4,128)S(1)}, f32[4,4,4,512]{3,2,1,0:T(4,128)S(1)}, u32[]{:S(2)}, u32[]{:S(2)}) collective-permute-start(f32[4,4,4,512]{3,2,1,0:T(4,128)S(1)} %get-tuple-element.13), channel_id=1, source_target_pairs={{1,2},{2,1},{3,4},{4,3},{5,6},{6,5},{7,8},{8,7},{9,10},{10,9},{11,... | collective-permute-start | bytes 393224 | tf_op jit(solution)/shard_map/ppermute | solution.py:318

commit v2 on v1

--- a/solution.py
+++ b/solution.py
@@ -179,7 +179,7 @@
                 outer[c, k, :, lanes] = jnp.where(odd, high, low)
 
 
-def main_kernel(offs, vids, got, absorb_part, emit_part, w, main, shifted):
+def main_kernel(offs, vids, got, absorb_part, emit_part, w, main, image, shifted):
     views, channels, rows, cols = w.shape
     slabs = main.shape[1]
     tiles = cols // LANES
@@ -188,6 +188,10 @@
     moves = [[offs[k, vids[v]] for k in range(slabs)] for v in range(views)]
     for t in range(tiles):
         lanes = pl.ds(t * LANES, LANES)
+        for v in range(views):
+            for b in range(bands):
+                for c in range(channels):
+                    image[v, c, 8 * b : 8 * b + 8, lanes] = got[v * bands + b, 2 + c, t]
         for v in range(views):
             grads = pixel_grads(got, absorb_part, emit_part, w, v, t, bands, slabs)
             for k, parts in grads:
@@ -202,22 +206,13 @@
                 )
 
 
-def join_kernel(strip, main, inner, outer, shown, out, image):
+def join_kernel(strip, main, inner, outer, out):
     rows = main.shape[2]
-    views, channels, _, cols = image.shape
-    bands = rows // 8
     odd = lax.rem(strip[0], 2) == 1
     near, far = inner[...], outer[...]
     out[:, :, 0:4, :] = main[:, :, 0:4, :] + jnp.where(odd, near, far)
     out[:, :, 4 : rows - 4, :] = main[:, :, 4 : rows - 4, :]
     out[:, :, rows - 4 :, :] = main[:, :, rows - 4 :, :] + jnp.where(odd, far, near)
-    for v in range(views):
-        for b in range(bands):
-            for t in range(cols // LANES):
-                for c in range(channels):
-                    image[v, c, 8 * b : 8 * b + 8, t * LANES : (t + 1) * LANES] = shown[
-                        v * bands + b, 2 + c, t
-                    ]
 
 
 def off_chip(x):
@@ -299,7 +294,6 @@
         name="scan",
     )(place, agg, *parts, w)
     got = on_chip(swap(sent, near))
-    shown = got
 
     to_inner, to_outer = pl.pallas_call(
         edge_kernel,
@@ -317,25 +311,25 @@
     )(table, view_ids, strip, got, on_chip(absorb_part), on_chip(emit_part), w)
     from_outer = lax.ppermute(to_outer, "lat", links)
     from_inner = lax.ppermute(to_inner, "lat", pairs)
-    main = pl.pallas_call(
+    main, image_out = pl.pallas_call(
         main_kernel,
-        out_shape=kept(channels, slabs, rows, cols),
+        out_shape=(kept(channels, slabs, rows, cols), f32(views, channels, rows, cols)),
         in_specs=[SMEM, SMEM, VMEM, VMEM, VMEM, VMEM],
-        out_specs=VMEM,
+        out_specs=(VMEM, VMEM),
         scratch_shapes=[
             pltpu.VMEM((views, slabs, channels, tiles, rows + 16, LANES), jnp.float32)
         ],
         compiler_params=LIMIT,
         name="main",
     )(table, view_ids, got, on_chip(absorb_part), on_chip(emit_part), w)
-    grad_out, image_out = pl.pallas_call(
+    grad_out = pl.pallas_call(
         join_kernel,
-        out_shape=(f32(channels, slabs, rows, cols), f32(views, channels, rows, cols)),
-        in_specs=[SMEM, VMEM, VMEM, VMEM, VMEM],
-        out_specs=(VMEM, VMEM),
+        out_shape=f32(channels, slabs, rows, cols),
+        in_specs=[SMEM, VMEM, VMEM, VMEM],
+        out_specs=VMEM,
         compiler_params=LIMIT,
         name="join",
-    )(strip, on_chip(main), on_chip(from_inner), on_chip(from_outer), on_chip(shown))
+    )(strip, on_chip(main), on_chip(from_inner), on_chip(from_outer))
     return (image_out, grad_out)
 
 

time: 82.2 us -> 82.1 us (level)
  transfers between devices with their start and end apart: 7 -> 7, of which waited for: 4 -> 4; matrix products, arithmetic and copies ran while one was open for 0% -> 0% of each run, Pallas kernels for 1% -> 2%
where the time goes in v2:
time: 82.1 us; the launch traced here: 81.7 us
  starting transfers between devices  28.5 us (35%)
  blocking collectives  27.6 us (34%)
  waiting for transfers between devices  19.2 us (23%)
  Pallas kernels  4.55 us (6%)
  other arithmetic  1.14 us (1%)
    all_to_all x2, blocking collectives, swap(): lax.all_to_all(x, 'depth', 0, 0, tiled=True, axis_index_groups=groups)  27.6 us
    ppermute x3, starting transfers between devices, on_device(): parts[j] = lax.ppermute(grouped, 'depth', hops)  17.7 us
    ppermute x3, waiting for transfers between devices, on_device(): parts[j] = lax.ppermute(grouped, 'depth', hops)  11.6 us
    ppermute x1, waiting for transfers between devices, on_device(): from_outer = lax.ppermute(to_outer, 'lat', links)  4.64 us
    ppermute x1, starting transfers between devices, on_device(): outer = lax.ppermute(jnp.where(odd, last, first), 'lat', links)  3.34 us
    ppermute x1, starting transfers between devices, on_device(): from_inner = lax.ppermute(to_inner, 'lat', pairs)  3.21 us
    ppermute x1, waiting for transfers between devices, on_device(): outer = lax.ppermute(jnp.where(odd, last, first), 'lat', links)  2.92 us
    ppermute x1, starting transfers between devices, on_device(): from_outer = lax.ppermute(to_outer, 'lat', links)  2.14 us
  transfers between devices with their start and end apart: 7, of which 4 were waited for; matrix products, arithmetic and copies ran while one was open for 0% of the time, Pallas kernels for 2%

profile of v2, /device:TPU:25, one launch (start us, length us, event | category | flops | bytes accessed | tf_op | source)
XLA Modules:
  0.0 81.7 jit_solution(229161216199117623)
XLA Ops:
  0.6 0.0 copy-start.1
  0.6 1.1 %slice_select_fusion = (f32[4,4,4,512]{3,2,1,0:T(4,128)S(1)}, f32[4,4,4,512]{3,2,1,0:T(4,128)S(1)}) fusion(f32[4,4,16,512]{3,2,1,0:T(8,128)} %vol.1, pred[]{:T(512)} %bitcast.3), kind=kLoop, calls=%fused_computation | loop fusion | flops 65536 | bytes 524289 | tf_op jit(solution)/shard_map/jit(_where)/select_n | solution.py:250
  1.8 3.3 %collective-permute-start.1 = (f32[4,4,4,512]{3,2,1,0:T(4,128)S(1)}, f32[4,4,4,512]{3,2,1,0:T(4,128)S(1)}, u32[]{:S(2)}, u32[]{:S(2)}) collective-permute-start(f32[4,4,4,512]{3,2,1,0:T(4,128)S(1)} %get-tuple-element.16), channel_id=1, source_target_pairs={{1,2},{2,1},{3,4},{4,3},{5,6},{6,5},{7,8},{8,7},{9,10},{10,9},{11,... | collective-permute-start | bytes 393224 | tf_op jit(solution)/shard_map/ppermute | solution.py:250
  5.1 0.0 copy-start
  5.1 2.1 %collective-permute-start = (f32[4,4,4,512]{3,2,1,0:T(4,128)S(1)}, f32[4,4,4,512]{3,2,1,0:T(4,128)S(1)}, u32[]{:S(2)}, u32[]{:S(2)}) collective-permute-start(f32[4,4,4,512]{3,2,1,0:T(4,128)S(1)} %get-tuple-element.17), channel_id=1, source_target_pairs={{0,1},{1,0},{2,3},{3,2},{4,5},{5,4},{6,7},{7,6},{8,9},{9,8},{10,11... | collective-permute-start | bytes 393224 | tf_op jit(solution)/shard_map/ppermute | solution.py:251
  7.2 0.0 copy-done.1
  7.3 2.9 %collective-permute-done.1.refs_5_ = f32[4,4,4,512]{3,2,1,0:T(4,128)S(1)} collective-permute-done((f32[4,4,4,512]{3,2,1,0:T(4,128)S(1)}, f32[4,4,4,512]{3,2,1,0:T(4,128)S(1)}, u32[]{:S(2)}, u32[]{:S(2)}) %collective-permute-start.1) | collective-permute-done | bytes 131104 | tf_op jit(solution)/shard_map/ppermute | solution.py:250
  10.2 0.0 collective-permute-done.refs_4_
  10.2 0.0 copy-done
  10.2 1.0 %slab.1 = (f32[4,4,4,8,128]{4,3,2,1,0:T(8,128)S(1)}, f32[4,4,4,32,128]{4,3,2,1,0:T(8,128)S(1)}, f32[2,4,4,16,128]{4,3,2,1,0:T(8,128)S(1)}, f32[2,4,4,16,128]{4,3,2,1,0:T(8,128)S(1)}) custom-call(s32[4,8]{1,0:T(4,128)} %bitcast.4, s32[2]{0:T(128)} %vids.3, s32[1]{0:T(128)} %bitcast.2.refs_2_.strip, ...), custom_call_target="tpu_custom_call", output_to_operand_aliasing={{1}: (6, {})} | custom-call | tf_op jit(solution)/shard_map/slab/pallas_call | solution.py:260
  11.2 13.9 %all_to_all.10.agg = f32[4,4,4,8,128]{4,3,2,1,0:T(8,128)S(1)} all-to-all(f32[4,4,4,8,128]{4,3,2,1,0:T(8,128)S(1)} %get-tuple-element.9), channel_id=1, replica_groups={{0,32,64,96},{128,160,192,224},{320,352,256,288},{448,480,384,416},{1,3..., dimensions={0} | all-to-all | bytes 524288 | tf_op jit(solution)/shard_map/all_to_all | solution.py:245
  25.0 7.1 %collective-permute-start.4 = (f32[4,4,8,128]{3,2,1,0:T(8,128)S(1)}, f32[4,4,8,128]{3,2,1,0:T(8,128)S(1)}, u32[]{:S(2)}, u32[]{:S(2)}) collective-permute-start(f32[4,4,8,128]{3,2,1,0:T(8,128)S(1)} %group.1.refs_0_), channel_id=1, source_target_pairs={{0,448},{32,480},{64,384},{96,416},{128,320},{160,352},{192,256},{... | collective-permute-start | bytes 196616 | tf_op jit(solution)/shard_map/ppermute | solution.py:286
  32.2 8.7 %collective-permute-start.3 = (f32[4,4,8,128]{3,2,1,0:T(8,128)S(1)}, f32[4,4,8,128]{3,2,1,0:T(8,128)S(1)}, u32[]{:S(2)}, u32[]{:S(2)}) collective-permute-start(f32[4,4,8,128]{3,2,1,0:T(8,128)S(1)} %group.1.refs_0_), channel_id=1, source_target_pairs={{0,320},{32,352},{64,256},{96,288},{128,448},{160,480},{192,384},{... | collective-permute-start | bytes 196616 | tf_op jit(solution)/shard_map/ppermute | solution.py:286
  40.9 1.9 %collective-permute-start.2 = (f32[4,4,8,128]{3,2,1,0:T(8,128)S(1)}, f32[4,4,8,128]{3,2,1,0:T(8,128)S(1)}, u32[]{:S(2)}, u32[]{:S(2)}) collective-permute-start(f32[4,4,8,128]{3,2,1,0:T(8,128)S(1)} %group.1.refs_0_), channel_id=1, source_target_pairs={{0,128},{32,160},{64,192},{96,224},{128,0},{160,32},{192,64},{224,... | collective-permute-start | bytes 196616 | tf_op jit(solution)/shard_map/ppermute | solution.py:286
  42.8 0.0 collective-permute-done.4.refs_3_
  42.8 2.1 %collective-permute-done.3.refs_2_ = f32[4,4,8,128]{3,2,1,0:T(8,128)S(1)} collective-permute-done((f32[4,4,8,128]{3,2,1,0:T(8,128)S(1)}, f32[4,4,8,128]{3,2,1,0:T(8,128)S(1)}, u32[]{:S(2)}, u32[]{:S(2)}) %collective-permute-start.3) | collective-permute-done | bytes 65568 | tf_op jit(solution)/shard_map/ppermute | solution.py:286
  44.9 9.5 %collective-permute-done.2.refs_1_ = f32[4,4,8,128]{3,2,1,0:T(8,128)S(1)} collective-permute-done((f32[4,4,8,128]{3,2,1,0:T(8,128)S(1)}, f32[4,4,8,128]{3,2,1,0:T(8,128)S(1)}, u32[]{:S(2)}, u32[]{:S(2)}) %collective-permute-start.2) | collective-permute-done | bytes 65568 | tf_op jit(solution)/shard_map/ppermute | solution.py:286
  54.4 0.1 scan.1
  54.5 13.7 %all_to_all.11.got = f32[4,6,4,8,128]{4,3,2,1,0:T(8,128)S(1)} all-to-all(f32[4,6,4,8,128]{4,3,2,1,0:T(8,128)S(1)} %scan.1), channel_id=1, replica_groups={{0,32,64,96},{128,160,192,224},{320,352,256,288},{448,480,384,416},{1,3..., dimensions={0} | all-to-all | bytes 786432 | tf_op jit(solution)/shard_map/all_to_all | solution.py:245
  68.2 0.9 %edge.1 = (f32[4,4,4,512]{3,2,1,0:T(4,128)S(1)}, f32[4,4,4,512]{3,2,1,0:T(4,128)S(1)}) custom-call(s32[4,8]{1,0:T(4,128)} %bitcast.5, s32[2]{0:T(128)} %vids.3, s32[1]{0:T(128)} %bitcast.2.refs_2_.strip, f32[4,6,4,8,128]{4,3,2,1,0:T(8,128)S(1)} %all_to_all.11.got, f32[2,4,4,16,128]{4,3,2,1,0:T(8,128)S(1)} %get-tuple-element.10.absorb_part, ...), custom_call_target="tpu_custom_call" | custom-call | tf_op jit(solution)/shard_map/edge/pallas_call | solution.py:298
  69.2 3.2 %collective-permute-start.5 = (f32[4,4,4,512]{3,2,1,0:T(4,128)S(1)}, f32[4,4,4,512]{3,2,1,0:T(4,128)S(1)}, u32[]{:S(2)}, u32[]{:S(2)}) collective-permute-start(f32[4,4,4,512]{3,2,1,0:T(4,128)S(1)} %get-tuple-element.14), channel_id=1, source_target_pairs={{0,1},{1,0},{2,3},{3,2},{4,5},{5,4},{6,7},{7,6},{8,9},{9,8},{10,11... | collective-permute-start | bytes 393224 | tf_op jit(solution)/shard_map/ppermute | solution.py:313
  72.4 2.1 %collective-permute-start.6 = (f32[4,4,4,512]{3,2,1,0:T(4,128)S(1)}, f32[4,4,4,512]{3,2,1,0:T(4,128)S(1)}, u32[]{:S(2)}, u32[]{:S(2)}) collective-permute-start(f32[4,4,4,512]{3,2,1,0:T(4,128)S(1)} %get-tuple-element.15), channel_id=1, source_target_pairs={{1,2},{2,1},{3,4},{4,3},{5,6},{6,5},{7,8},{8,7},{9,10},{10,9},{11,... | collective-permute-start | bytes 393224 | tf_op jit(solution)/shard_map/ppermute | solution.py:312
  74.5 1.6 %main.1 = (f32[4,4,16,512]{3,2,1,0:T(8,128)S(1)}, f32[2,4,16,512]{3,2,1,0:T(8,128)}) custom-call(s32[4,8]{1,0:T(4,128)} %bitcast.6, s32[2]{0:T(128)} %vids.3, f32[4,6,4,8,128]{4,3,2,1,0:T(8,128)S(1)} %all_to_all.11.got, f32[2,4,4,16,128]{4,3,2,1,0:T(8,128)S(1)} %get-tuple-element.10.absorb_part, f32[2,4,4,16,128]{4,3,2,1,0:T(8,128)S(1)} %get-tuple-element.11.emit_part, ...), custom_call_target="tpu_custom_call" | custom-call | tf_op jit(solution)/shard_map/main/pallas_call | solution.py:314
  76.1 0.0 collective-permute-done.5.inner
  76.1 4.6 %collective-permute-done.6.outer = f32[4,4,4,512]{3,2,1,0:T(4,128)S(1)} collective-permute-done((f32[4,4,4,512]{3,2,1,0:T(4,128)S(1)}, f32[4,4,4,512]{3,2,1,0:T(4,128)S(1)}, u32[]{:S(2)}, u32[]{:S(2)}) %collective-permute-start.6) | collective-permute-done | bytes 131104 | tf_op jit(solution)/shard_map/ppermute | solution.py:312
  80.8 0.9 %join.1 = f32[4,4,16,512]{3,2,1,0:T(8,128)} custom-call(s32[1]{0:T(128)} %bitcast.2.refs_2_.strip, f32[4,4,16,512]{3,2,1,0:T(8,128)S(1)} %get-tuple-element.13.main, f32[4,4,4,512]{3,2,1,0:T(4,128)S(1)} %collective-permute-done.5.inner, f32[4,4,4,512]{3,2,1,0:T(4,128)S(1)} %collective-permute-done.6.outer), custom_call_target="tpu_custom_call" | custom-call | tf_op jit(solution)/shard_map/join/pallas_call | solution.py:325
  (2 shorter events, 0.1 us)
Async XLA Ops:
  0.6 6.6 %copy-start.1 = (f32[4,4,16,512]{3,2,1,0:T(8,128)S(1)}, f32[4,4,16,512]{3,2,1,0:T(8,128)}, u32[]{:S(2)}) copy-start(f32[4,4,16,512]{3,2,1,0:T(8,128)} %vol.1) | copy-start | bytes 1572868
  1.8 8.4 %collective-permute-start.1 = (f32[4,4,4,512]{3,2,1,0:T(4,128)S(1)}, f32[4,4,4,512]{3,2,1,0:T(4,128)S(1)}, u32[]{:S(2)}, u32[]{:S(2)}) collective-permute-start(f32[4,4,4,512]{3,2,1,0:T(4,128)S(1)} %get-tuple-element.16), channel_id=1, source_target_pairs={{1,2},{2,1},{3,4},{4,3},{5,6},{6,5},{7,8},{8,7},{9,10},{10,9},{11,... | collective-permute-start | bytes 393224 | tf_op jit(solution)/shard_map/ppermute | solution.py:250
  5.1 5.1 %copy-start = (f32[2,4,16,512]{3,2,1,0:T(8,128)S(1)}, f32[2,4,16,512]{3,2,1,0:T(8,128)}, u32[]{:S(2)}) copy-start(f32[2,4,16,512]{3,2,1,0:T(8,128)} %w.3) | copy-start | bytes 786436
  5.1 5.0 %collective-permute-start = (f32[4,4,4,512]{3,2,1,0:T(4,128)S(1)}, f32[4,4,4,512]{3,2,1,0:T(4,128)S(1)}, u32[]{:S(2)}, u32[]{:S(2)}) collective-permute-start(f32[4,4,4,512]{3,2,1,0:T(4,128)S(1)} %get-tuple-element.17), channel_id=1, source_target_pairs={{0,1},{1,0},{2,3},{3,2},{4,5},{5,4},{6,7},{7,6},{8,9},{9,8},{10,11... | collective-permute-start | bytes 393224 | tf_op jit(solution)/shard_map/ppermute | solution.py:251
  25.0 17.8 %collective-permute-start.4 = (f32[4,4,8,128]{3,2,1,0:T(8,128)S(1)}, f32[4,4,8,128]{3,2,1,0:T(8,128)S(1)}, u32[]{:S(2)}, u32[]{:S(2)}) collective-permute-start(f32[4,4,8,128]{3,2,1,0:T(8,128)S(1)} %group.1.refs_0_), channel_id=1, source_target_pairs={{0,448},{32,480},{64,384},{96,416},{128,320},{160,352},{192,256},{... | collective-permute-start | bytes 196616 | tf_op jit(solution)/shard_map/ppermute | solution.py:286
  32.2 12.7 %collective-permute-start.3 = (f32[4,4,8,128]{3,2,1,0:T(8,128)S(1)}, f32[4,4,8,128]{3,2,1,0:T(8,128)S(1)}, u32[]{:S(2)}, u32[]{:S(2)}) collective-permute-start(f32[4,4,8,128]{3,2,1,0:T(8,128)S(1)} %group.1.refs_0_), channel_id=1, source_target_pairs={{0,320},{32,352},{64,256},{96,288},{128,448},{160,480},{192,384},{... | collective-permute-start | bytes 196616 | tf_op jit(solution)/shard_map/ppermute | solution.py:286
  40.9 13.5 %collective-permute-start.2 = (f32[4,4,8,128]{3,2,1,0:T(8,128)S(1)}, f32[4,4,8,128]{3,2,1,0:T(8,128)S(1)}, u32[]{:S(2)}, u32[]{:S(2)}) collective-permute-start(f32[4,4,8,128]{3,2,1,0:T(8,128)S(1)} %group.1.refs_0_), channel_id=1, source_target_pairs={{0,128},{32,160},{64,192},{96,224},{128,0},{160,32},{192,64},{224,... | collective-permute-start | bytes 196616 | tf_op jit(solution)/shard_map/ppermute | solution.py:286
  69.2 7.0 %collective-permute-start.5 = (f32[4,4,4,512]{3,2,1,0:T(4,128)S(1)}, f32[4,4,4,512]{3,2,1,0:T(4,128)S(1)}, u32[]{:S(2)}, u32[]{:S(2)}) collective-permute-start(f32[4,4,4,512]{3,2,1,0:T(4,128)S(1)} %get-tuple-element.14), channel_id=1, source_target_pairs={{0,1},{1,0},{2,3},{3,2},{4,5},{5,4},{6,7},{7,6},{8,9},{9,8},{10,11... | collective-permute-start | bytes 393224 | tf_op jit(solution)/shard_map/ppermute | solution.py:313
  72.4 8.4 %collective-permute-start.6 = (f32[4,4,4,512]{3,2,1,0:T(4,128)S(1)}, f32[4,4,4,512]{3,2,1,0:T(4,128)S(1)}, u32[]{:S(2)}, u32[]{:S(2)}) collective-permute-start(f32[4,4,4,512]{3,2,1,0:T(4,128)S(1)} %get-tuple-element.15), channel_id=1, source_target_pairs={{1,2},{2,1},{3,4},{4,3},{5,6},{6,5},{7,8},{8,7},{9,10},{10,9},{11,... | collective-permute-start | bytes 393224 | tf_op jit(solution)/shard_map/ppermute | solution.py:312
